TPU v7x, 32 devices: a whole 2x2x4 slice. The times are simulated.
32 devices in a mesh: chi: 4 (over y, x), dl: 4 (over z), cell: 2 (over core).
Axes of the slice: x: 2, y: 2, z: 4, core: 2. Of those that a mesh axis runs over, the one named last changes fastest.
Arguments:
- left_env: bfloat16 [2, 512, 512, 36], P('cell', None, 'chi'), may hold values from -6 to 6
- up_left: bfloat16 [2, 512, 36, 512], P('cell', 'chi', None, 'dl'), may hold values from -0.109375 to 0.109375
- up_center: bfloat16 [2, 512, 36, 512], P('cell', 'chi', None, 'dl'), may hold values from -0.109375 to 0.109375
- right_env: bfloat16 [2, 512, 36, 512], P('cell', 'dl'), may hold values from -0.046875 to 0.046875
- center: bfloat16 [2, 512, 512], P('cell', None, 'dl'), may hold values from -0.25 to 0.25
- ket_tensor: bfloat16 [2, 6, 6, 6, 6, 2], P('cell'), may hold values from -0.875 to 0.875
Outputs:
- left_env_new: float32 [2, 512, 36, 512], P('cell', 'chi', None, 'dl')
- new_left: float32 [2, 512, 36, 512], P('cell', 'chi', None, 'dl')
All inputs are finite; a program needn't handle non-finite values.
Results may differ from a plain program's by a relative error of at most 0.0066.
The roundings to bfloat16 on the way count: a program that leaves them out, or rounds other values in their place, can miss the bound.
Values may be sent and summed in bfloat16 or wider, within the bound.
A program may use at most 256 MiB of HBM per device.

v0:
```python
from functools import partial
import math

import jax
import jax.numpy as jnp
from jax import lax
from jax.sharding import PartitionSpec as P

ITERS = 5


HIGHEST = lax.Precision.HIGHEST


def from_behind(block, axis, distance):
    devices = range(lax.axis_size(axis))
    route = [((i - distance) % len(devices), i) for i in devices]
    return lax.ppermute(block, axis, route)


def layered(block, tensor):
    leg_size = tensor.shape[0]
    amount = block.shape[0]
    columns = block.shape[3]
    unfolded = block.reshape(amount, leg_size, leg_size, leg_size, leg_size, columns)
    ket_side = jnp.einsum(
        "blLuUc,lurdp->bLUcrdp", unfolded, tensor, preferred_element_type=jnp.float32
    ).astype(jnp.bfloat16)
    both_sides = jnp.einsum(
        "bLUcrdp,LUsep->brsdec", ket_side, tensor, preferred_element_type=jnp.float32
    )
    return both_sides.reshape(amount, leg_size * leg_size, leg_size * leg_size, columns).astype(
        jnp.bfloat16
    )


def through_site(stacked, tensor):
    amount = stacked.shape[0]
    stride = min(amount, 8)
    blocks = stacked.reshape((amount // stride, stride) + stacked.shape[1:])
    finished = lax.map(partial(layered, tensor=tensor), blocks)
    return finished.reshape((amount,) + finished.shape[2:])


def shards(left_env, up_left, up_center, right_env, center, ket_tensor):
    env_local = left_env[0]
    left_iso = up_left[0]
    left_mid = up_center[0]
    env_right = right_env[0]
    bond_mat = center[0]
    site_ket = ket_tensor[0]
    chi_all = env_local.shape[0]
    leg_width = env_local.shape[2]
    col_count = left_iso.shape[2]
    iso_all, mid_all = (
        lax.all_gather(left_iso, "chi", axis=0, tiled=True),
        lax.all_gather(left_mid, "chi", axis=0, tiled=True),
    )
    left_sum = jnp.einsum("abm,asc->bmsc", env_local, iso_all, preferred_element_type=jnp.float32)
    left_cut = through_site(left_sum.astype(jnp.bfloat16), site_ket)
    right_sum = jnp.einsum("abm,asc->bmsc", env_local, mid_all, preferred_element_type=jnp.float32)
    right_cut = through_site(right_sum.astype(jnp.bfloat16), site_ket)
    next_iso = from_behind(left_iso, "cell", -1)
    bra_iso = lax.all_gather(next_iso, "dl", axis=2, tiled=True)
    env_new = lax.psum_scatter(
        jnp.einsum("bmdc,bdk->kmc", left_cut, bra_iso, preferred_element_type=jnp.float32),
        "chi",
        scatter_dimension=0,
        tiled=True,
    )
    center_term = jnp.einsum(
        "bmda,amc->cbd", right_cut, env_right, preferred_element_type=jnp.float32
    )
    mixed = jnp.einsum(
        "abm,ax->bmx", env_local, bond_mat, preferred_element_type=jnp.float32
    ).astype(jnp.bfloat16)
    bond_term = jnp.einsum("bma,amc->cb", mixed, env_right, preferred_element_type=jnp.float32)
    center_part, bond_part = (
        lax.psum_scatter(center_term, "dl", scatter_dimension=0, tiled=True),
        lax.psum_scatter(bond_term, "dl", scatter_dimension=0, tiled=True),
    )
    center_all, bond_cols = (
        lax.all_gather(center_part.astype(jnp.bfloat16), "dl", axis=0, tiled=True),
        lax.all_gather(bond_part.astype(jnp.bfloat16), "dl", axis=0, tiled=True),
    )
    bond_full = lax.all_gather(bond_cols, "chi", axis=1, tiled=True)
    bond_mine = lax.dynamic_slice_in_dim(bond_full, lax.axis_index("dl") * col_count, col_count, 1)
    target = jnp.einsum("cbd,cx->bdx", center_all, bond_mine, preferred_element_type=jnp.float32)
    factor = 0.25 * math.sqrt(chi_all)
    norm_sum = lax.psum(jnp.sum(target * target), ("chi", "dl"))
    current = target * (factor / jnp.sqrt(norm_sum))
    for sweep_index in range(ITERS):
        spread = lax.all_gather(current.astype(jnp.bfloat16), "dl", axis=2, tiled=True).astype(
            current.dtype
        )
        gram_rows = lax.psum(
            jnp.einsum("bdx,bdy->xy", current, spread, precision=HIGHEST).astype(jnp.bfloat16),
            "chi",
        ).astype(jnp.float32)
        current = 1.5 * current - 0.5 * jnp.einsum(
            "bdy,xy->bdx", spread, gram_rows, precision=HIGHEST
        )
    new_left = current * math.sqrt(chi_all * leg_width)
    return (env_new[None], new_left[None])


def solution(mesh):
    placed = (
        P("cell", None, "chi", None),
        P("cell", "chi", None, "dl"),
        P("cell", "chi", None, "dl"),
        P("cell", "dl", None, None),
        P("cell", None, "dl"),
        P("cell", None, None, None, None, None),
    )
    return jax.shard_map(
        shards,
        mesh=mesh,
        in_specs=placed,
        out_specs=(P("cell", "chi", None, "dl"), P("cell", "chi", None, "dl")),
        check_vma=False,
    )
```

profile of v0, /device:TPU:0, one launch (start us, length us, event | category | flops | bytes accessed | tf_op | source)
XLA Modules:
  0.0 1720.3 jit_solution(1469185994787700763)
XLA Ops:
  9.4 60.3 %all-gather.28.cloned.1.call-done = bf16[1,512,36,128]{3,1,2,0:T(8,128)(2,1)} async-done(((bf16[1,128,36,128]{3,1,2,0:T(8,128)(2,1)}), bf16[1,512,36,128]{3,1,2,0:T(8,128)(2,1)}) %all-gather.28.cloned.1.call-update) | async-done | bytes 4718608 | tf_op jit(solution)/shard_map/all_gather | solution.py:57
  69.7 29.6 %convert_bitcast_fusion = bf16[16,8,36,36,128]{4,1,0,3,2:T(8,128)(2,1)} fusion(bf16[1,512,128,36]{2,1,3,0:T(8,128)(2,1)} %param.10, bf16[1,512,36,128]{3,1,2,0:T(8,128)(2,1)} %all-gather.28.cloned.1.call-done), kind=kOutput, calls=%fused_computation.26 | convolution fusion | flops 21764505600 | bytes 51904512 | tf_op jit(solution)/shard_map/abm,asc->bmsc/dot_general | solution.py:61
  99.2 14.1 broadcast.9.clone2.1
  113.3 220.6 %while.21 = (s32[]{:T(128)}, bf16[16,8,36,36,128]{4,1,0,3,2:T(8,128)(2,1)}, bf16[16,8,36,36,128]{4,1,0,3,2:T(8,128)(2,1)}, bf16[6,6,6,6,2]{1,3,4,0,2:T(8,128)(2,1)S(1)}, s32[]{:T(128)}) while((s32[]{:T(128)}, bf16[16,8,36,36,128]{4,1,0,3,2:T(8,128)(2,1)}, bf16[16,8,36,36,128]{4,1,0,3,2:T(8,128)(2,1)}, bf16[6,6,6,6,2]{1,3,4,0,2:T(8,128)(2,1)S(1)}, ...), condition=%wide.region_4.5_spmd, body=%wide.region_3.4_spmd.sunk | while | flops 386187264 | bytes 31861440 | solution.py:41
  117.9 4.3 fusion.122
  131.7 4.3 fusion.122
  145.6 4.3 fusion.122
  159.4 4.3 fusion.122
  173.2 4.3 fusion.122
  186.9 4.3 fusion.122
  200.7 4.3 fusion.122
  214.5 4.3 fusion.122
  228.3 4.3 fusion.122
  242.1 4.3 fusion.122
  255.9 4.3 fusion.122
  269.7 4.3 fusion.122
  283.5 4.3 fusion.122
  297.3 4.3 fusion.122
  311.0 4.3 fusion.122
  324.8 4.3 fusion.122
  334.0 28.7 %fusion.37 = f32[512,128,36]{0,1,2:T(8,128)} fusion(bf16[1,128,36,512]{3,1,2,0:T(8,128)(2,1)} %param.13, bf16[16,8,36,36,128]{4,1,0,3,2:T(8,128)(2,1)} %get-tuple-element.47), kind=kOutput, calls=%fused_computation.39 | convolution fusion | flops 21743271936 | bytes 56623104 | tf_op jit(solution)/shard_map/bmda,amc->cbd/dot_general | solution.py:71
  362.7 7.2 fusion.51
  370.0 154.1 %reduce-scatter.6.cloned.1.call-done = f32[128,128,36]{0,1,2:T(8,128)} async-done(((f32[512,128,36]{0,1,2:T(8,128)}), f32[128,128,36]{0,1,2:T(8,128)}) %reduce-scatter.6.cloned.1.call-update) | async-done | bytes 2359312 | tf_op jit(solution)/shard_map/reduce_scatter | solution.py:79
  527.1 20.4 %reduce-scatter.8.cloned.1.call-done = f32[128,128]{0,1:T(8,128)} async-done(((f32[512,128]{0,1:T(8,128)}), f32[128,128]{0,1:T(8,128)}) %reduce-scatter.8.cloned.1.call-update) | async-done | bytes 65552 | tf_op jit(solution)/shard_map/reduce_scatter | solution.py:80
  548.3 12.3 all_gather.37
  560.6 10.0 all_gather.38
  570.6 68.1 %all-gather.14.cloned.1.call-done = bf16[512,128,36]{0,1,2:T(8,128)(2,1)} async-done(((bf16[128,128,36]{0,1,2:T(8,128)(2,1)}), bf16[512,128,36]{0,1,2:T(8,128)(2,1)}) %all-gather.14.cloned.1.call-update) | async-done | bytes 4718608 | tf_op jit(solution)/shard_map/all_gather | solution.py:83
  638.8 4.3 multiply_reduce_fusion
  643.1 38.9 %psum.42 = f32[]{:T(128)} all-reduce(f32[]{:T(128)} %get-tuple-element.94), channel_id=1, replica_groups=mesh['chi'=4,'dl'=4,'cell'=2] {'chi','dl'}, use_global_device_ids=true, to_apply=%region_8.9 | all-reduce | flops 1 | bytes 8 | tf_op jit(solution)/shard_map/psum | solution.py:90
  684.1 86.6 %all-gather.16.cloned.1.call-done = bf16[128,36,512]{2,0,1:T(8,128)(2,1)} async-done(((bf16[128,36,128]{2,0,1:T(8,128)(2,1)}), bf16[128,36,512]{2,0,1:T(8,128)(2,1)}) %all-gather.16.cloned.1.call-update) | async-done | bytes 4718608 | tf_op jit(solution)/shard_map/all_gather | solution.py:93
  770.7 5.5 fusion.58
  776.2 40.3 %all-reduce.6.cloned.1.call-done = bf16[128,512]{1,0:T(8,128)(2,1)} async-done(((bf16[128,512]{1,0:T(8,128)(2,1)}), bf16[128,512]{1,0:T(8,128)(2,1)}) %all-reduce.6.cloned.1.call-update) | async-done | bytes 131088 | tf_op jit(solution)/shard_map/psum | solution.py:96
  816.5 5.5 fusion.74
  822.3 89.0 %all-gather.18.cloned.1.call-done = bf16[128,36,512]{2,0,1:T(8,128)(2,1)} async-done(((bf16[128,36,128]{2,0,1:T(8,128)(2,1)}), bf16[128,36,512]{2,0,1:T(8,128)(2,1)}) %all-gather.18.cloned.1.call-update) | async-done | bytes 4718608 | tf_op jit(solution)/shard_map/all_gather | solution.py:93
  911.4 6.2 fusion.54
  917.6 40.3 %all-reduce.8.cloned.1.call-done = bf16[128,512]{1,0:T(8,128)(2,1)} async-done(((bf16[128,512]{1,0:T(8,128)(2,1)}), bf16[128,512]{1,0:T(8,128)(2,1)}) %all-reduce.8.cloned.1.call-update) | async-done | bytes 131088 | tf_op jit(solution)/shard_map/psum | solution.py:96
  957.9 5.5 fusion.75
  963.5 89.2 %all-gather.20.cloned.1.call-done = bf16[128,36,512]{2,0,1:T(8,128)(2,1)} async-done(((bf16[128,36,128]{2,0,1:T(8,128)(2,1)}), bf16[128,36,512]{2,0,1:T(8,128)(2,1)}) %all-gather.20.cloned.1.call-update) | async-done | bytes 4718608 | tf_op jit(solution)/shard_map/all_gather | solution.py:93
  1052.7 6.2 fusion.55
  1059.0 40.3 %all-reduce.10.cloned.1.call-done = bf16[128,512]{1,0:T(8,128)(2,1)} async-done(((bf16[128,512]{1,0:T(8,128)(2,1)}), bf16[128,512]{1,0:T(8,128)(2,1)}) %all-reduce.10.cloned.1.call-update) | async-done | bytes 131088 | tf_op jit(solution)/shard_map/psum | solution.py:96
  1099.3 5.6 fusion.76
  1105.6 88.6 %all-gather.22.cloned.1.call-done = bf16[128,36,512]{2,0,1:T(8,128)(2,1)} async-done(((bf16[128,36,128]{2,0,1:T(8,128)(2,1)}), bf16[128,36,512]{2,0,1:T(8,128)(2,1)}) %all-gather.22.cloned.1.call-update) | async-done | bytes 4718608 | tf_op jit(solution)/shard_map/all_gather | solution.py:93
  1194.1 5.5 fusion.56
  1200.6 50.5 %all-gather.26.cloned.1.call-done = bf16[1,512,36,128]{3,1,2,0:T(8,128)(2,1)} async-done(((bf16[1,128,36,128]{3,1,2,0:T(8,128)(2,1)}), bf16[1,512,36,128]{3,1,2,0:T(8,128)(2,1)}) %all-gather.26.cloned.1.call-update) | async-done | bytes 4718608 | tf_op jit(solution)/shard_map/all_gather | solution.py:56
  1251.1 29.6 %convert_bitcast_fusion.1 = bf16[16,8,36,36,128]{4,1,0,3,2:T(8,128)(2,1)} fusion(bf16[1,512,128,36]{2,1,3,0:T(8,128)(2,1)} %param.10, bf16[1,512,36,128]{3,1,2,0:T(8,128)(2,1)} %all-gather.26.cloned.1.call-done), kind=kOutput, calls=%fused_computation.27 | convolution fusion | flops 21764505600 | bytes 51904512 | tf_op jit(solution)/shard_map/abm,asc->bmsc/dot_general | solution.py:59
  1280.7 15.9 all-reduce.12.cloned.1.call-done
  1296.6 5.5 fusion.77
  1302.4 14.7 broadcast.9.clone2
  1317.1 220.8 %while.20 = (s32[]{:T(128)}, bf16[16,8,36,36,128]{4,1,0,3,2:T(8,128)(2,1)}, bf16[16,8,36,36,128]{4,1,0,3,2:T(8,128)(2,1)}, bf16[6,6,6,6,2]{1,3,4,0,2:T(8,128)(2,1)S(1)}, s32[]{:T(128)}) while((s32[]{:T(128)}, bf16[16,8,36,36,128]{4,1,0,3,2:T(8,128)(2,1)}, bf16[16,8,36,36,128]{4,1,0,3,2:T(8,128)(2,1)}, bf16[6,6,6,6,2]{1,3,4,0,2:T(8,128)(2,1)S(1)}, ...), condition=%wide.region_1.2_spmd, body=%wide.region_0.1_spmd.sunk | while | flops 386187264 | bytes 31861440 | solution.py:41
  1321.7 4.3 fusion.115
  1335.5 4.3 fusion.115
  1349.3 4.3 fusion.115
  1363.2 4.3 fusion.115
  1376.9 4.3 fusion.115
  1404.5 4.3 fusion.115
  1432.1 4.3 fusion.115
  1459.8 4.3 fusion.115
  1473.6 4.3 fusion.115
  1487.4 4.3 fusion.115
  1537.9 29.8 %fusion.32 = f32[512,36,128]{0,2,1:T(8,128)} fusion(bf16[128,36,512]{2,0,1:T(8,128)(2,1)} %all-gather.12.cloned.1.call-done, bf16[16,8,36,36,128]{4,1,0,3,2:T(8,128)(2,1)} %get-tuple-element.46), kind=kOutput, calls=%fused_computation.38 | convolution fusion | flops 21743271936 | bytes 56623104 | tf_op jit(solution)/shard_map/bmdc,bdk->kmc/dot_general | solution.py:66
  1569.3 5.4 fusion.57
  1574.8 88.0 %reduce-scatter.4.cloned.1.call-done = f32[128,36,128]{0,2,1:T(8,128)} async-done(((f32[512,36,128]{0,2,1:T(8,128)}), f32[128,36,128]{0,2,1:T(8,128)}) %reduce-scatter.4.cloned.1.call-update) | async-done | bytes 2359312 | tf_op jit(solution)/shard_map/reduce_scatter | solution.py:65
  1665.9 42.5 %all-reduce.14.cloned.1.call-done = bf16[128,512]{1,0:T(8,128)(2,1)} async-done(((bf16[128,512]{1,0:T(8,128)(2,1)}), bf16[128,512]{1,0:T(8,128)(2,1)}) %all-reduce.14.cloned.1.call-update) | async-done | bytes 131088 | tf_op jit(solution)/shard_map/psum | solution.py:96
  1708.4 5.1 multiply_bitcast_fusion
  (185 shorter events, 343.2 us)
Async XLA Ops:
  7.2 355.5 %copy-start = (bf16[1,512,128]{2,1,0:T(8,128)(2,1)S(1)}, bf16[1,512,128]{2,1,0:T(8,128)(2,1)}, u32[]{:S(2)}) copy-start(bf16[1,512,128]{2,1,0:T(8,128)(2,1)} %param.14) | copy-start | bytes 393220
  7.2 62.5 %all-gather.28.cloned.1.call-start = ((), (), s32[]{:S(2)}) async-start(), calls=%async_computation.19 | async-start | bytes 5898240 | tf_op jit(solution)/shard_map/all_gather | solution.py:57
  7.9 516.2 %reduce-scatter.6.cloned.1.call-start = ((), (), s32[]{:S(2)}) async-start(), calls=%async_computation.5 | async-start | bytes 11796480 | tf_op jit(solution)/shard_map/reduce_scatter | solution.py:79
  362.7 184.8 %reduce-scatter.8.cloned.1.call-start = ((), (), s32[]{:S(2)}) async-start(), calls=%async_computation.7 | async-start | bytes 327680 | tf_op jit(solution)/shard_map/reduce_scatter | solution.py:80
  370.0 268.8 %all-gather.14.cloned.1.call-start = ((), (), s32[]{:S(2)}) async-start(), calls=%async_computation.6 | async-start | bytes 5898240 | tf_op jit(solution)/shard_map/all_gather | solution.py:83
  527.0 243.7 %all-gather.16.cloned.1.call-start = ((), (), s32[]{:S(2)}) async-start(), calls=%async_computation.8 | async-start | bytes 5898240 | tf_op jit(solution)/shard_map/all_gather | solution.py:93
  684.1 132.4 %all-reduce.6.cloned.1.call-start = ((), (), s32[]{:S(2)}) async-start(), calls=%async_computation.9 | async-start | bytes 262144 | tf_op jit(solution)/shard_map/psum | solution.py:96
  776.2 135.2 %all-gather.18.cloned.1.call-start = ((), (), s32[]{:S(2)}) async-start(), calls=%async_computation.10 | async-start | bytes 5898240 | tf_op jit(solution)/shard_map/all_gather | solution.py:93
  822.0 135.8 %copy-start.3 = (f32[128,36,128]{2,0,1:T(8,128)S(1)}, f32[128,36,128]{2,0,1:T(8,128)}, u32[]{:S(2)}) copy-start(f32[128,36,128]{2,0,1:T(8,128)} %get-tuple-element.97) | copy-start | bytes 7077892
  822.1 135.8 %all-reduce.8.cloned.1.call-start = ((), (), s32[]{:S(2)}) async-start(), calls=%async_computation.11 | async-start | bytes 262144 | tf_op jit(solution)/shard_map/psum | solution.py:96
  917.5 135.2 %all-gather.20.cloned.1.call-start = ((), (), s32[]{:S(2)}) async-start(), calls=%async_computation.12 | async-start | bytes 5898240 | tf_op jit(solution)/shard_map/all_gather | solution.py:93
  963.4 135.8 %all-reduce.10.cloned.1.call-start = ((), (), s32[]{:S(2)}) async-start(), calls=%async_computation.13 | async-start | bytes 262144 | tf_op jit(solution)/shard_map/psum | solution.py:96
  1058.9 135.2 %all-gather.22.cloned.1.call-start = ((), (), s32[]{:S(2)}) async-start(), calls=%async_computation.14 | async-start | bytes 5898240 | tf_op jit(solution)/shard_map/all_gather | solution.py:93
  1104.8 146.3 %all-gather.26.cloned.1.call-start = ((), (), s32[]{:S(2)}) async-start(), calls=%async_computation.18 | async-start | bytes 5898240 | tf_op jit(solution)/shard_map/all_gather | solution.py:56
  1105.4 191.2 %all-reduce.12.cloned.1.call-start = ((), (), s32[]{:S(2)}) async-start(), calls=%async_computation.15 | async-start | bytes 262144 | tf_op jit(solution)/shard_map/psum | solution.py:96
  1105.5 94.2 %collective-permute-start = (bf16[128,36,128]{2,0,1:T(8,128)(2,1)}, bf16[128,36,128]{2,0,1:T(8,128)(2,1)}, u32[]{:S(2)}, u32[]{:S(2)}) collective-permute-start(bf16[128,36,128]{2,0,1:T(8,128)(2,1)} %bitcast.242), channel_id=1, source_target_pairs={{1,0},{0,1},{3,2},{2,3},{5,4},{4,5},{7,6},{6,7},{9,8},{8,9},{11,10... | collective-permute-start | bytes 3538952 | tf_op jit(solution)/shard_map/ppermute | solution.py:18
  1199.6 338.3 %all-gather.12.cloned.1.call-start = ((), (), s32[]{:S(2)}) async-start(), calls=%async_computation.3 | async-start | bytes 5898240 | tf_op jit(solution)/shard_map/all_gather | solution.py:64
  1200.2 367.8 %all-gather.24.cloned.1.call-start = ((), (), s32[]{:S(2)}) async-start(), calls=%async_computation.16 | async-start | bytes 5898240 | tf_op jit(solution)/shard_map/all_gather | solution.py:93
  1302.1 360.7 %reduce-scatter.4.cloned.1.call-start = ((), (), s32[]{:S(2)}) async-start(), calls=%async_computation.4 | async-start | bytes 11796480 | tf_op jit(solution)/shard_map/reduce_scatter | solution.py:65
  1567.7 1.7 copy-start.2
  1567.7 140.7 %all-reduce.14.cloned.1.call-start = ((), (), s32[]{:S(2)}) async-start(), calls=%async_computation.17 | async-start | bytes 262144 | tf_op jit(solution)/shard_map/psum | solution.py:96
  1662.8 50.7 %copy-start.1 = (bf16[1,512,128]{2,1,0:T(8,128)(2,1)S(1)}, bf16[1,512,128]{2,1,0:T(8,128)(2,1)}, u32[]{:S(2)}) copy-start(bf16[1,512,128]{2,1,0:T(8,128)(2,1)} %param.14) | copy-start | bytes 393220
Sparse Core Ops, SparseCore 0:
  9.9 59.7 all-gather.27
  362.8 161.2 reduce-scatter.5
  527.0 20.4 reduce-scatter.7
  549.5 89.1 all-gather.13
  684.2 86.4 all-gather.15
  776.3 40.1 all-reduce.5
  822.2 89.1 all-gather.17
  917.7 40.1 all-reduce.7
  963.6 89.1 all-gather.19
  1059.0 40.1 all-reduce.9
  1105.0 89.1 all-gather.21
  1195.8 55.2 all-gather.25
  1254.6 41.9 all-reduce.11
  1298.1 89.1 all-gather.11
  1389.3 87.3 all-gather.23
  1567.8 94.9 reduce-scatter.3
  1666.4 41.9 all-reduce.13
where the time goes:
time: 1730 us; the launch traced here: 1720 us
  waiting for transfers between devices  976 us (56%)
  matrix products  408 us (24%)
  local copies, waits for them, and re-layouts  252 us (15%)
  blocking collectives  61.2 us (4%)
    all_gather x5, waiting for transfers between devices, shards(): lax.all_gather(current.astype(jnp.bfloat16), 'dl', axis=2, tiled=True)  353 us
    psum x5, waiting for transfers between devices, shards(): lax.psum(jnp.einsum('bdx,bdy->xy', current, spread, precision=HIGHEST).as...  179 us
    reduce_scatter x1, waiting for transfers between devices, shards(): lax.psum_scatter(center_term, 'dl', scatter_dimension=0, tiled=True)  154 us
    dot_general x32, matrix products, layered(): jnp.einsum('bLUcrdp,LUsep->brsdec', ket_side, tensor, preferred_element_t...  138 us
    convert_element_type x32, local copies, waits for them, and re-layouts, layered(): both_sides.reshape(amount, leg_size * leg_size, leg_size * leg_size, colu...  98.5 us
    reduce_scatter x1, waiting for transfers between devices, shards(): lax.psum_scatter(jnp.einsum('bmdc,bdk->kmc', left_cut, bra_iso, preferred...  88 us
    dot_general x32, matrix products, layered(): jnp.einsum('blLuUc,lurdp->bLUcrdp', unfolded, tensor, preferred_element_t...  84.9 us
    all_gather x1, waiting for transfers between devices, shards(): lax.all_gather(center_part.astype(jnp.bfloat16), 'dl', axis=0, tiled=True)  68.1 us
  transfers between devices with their start and end apart: 18, of which 15 were waited for; matrix products, arithmetic and copies ran while one was open for 19% of the time, Pallas kernels for 0%

commit v1 on v0

v1 whole, which is shorter than its diff:
```python
import math

import jax
import jax.numpy as jnp
from jax import lax
from jax.sharding import PartitionSpec as P

ITERS = 5


HIGH = lax.Precision.HIGH
F32 = jnp.float32
BF16 = jnp.bfloat16


def from_behind(block, axis, distance):
    devices = range(lax.axis_size(axis))
    route = [((i - distance) % len(devices), i) for i in devices]
    return lax.ppermute(block, axis, route)


def pick(rows, cols, row_of, col_of):
    r = lax.broadcasted_iota(jnp.int32, (rows, cols), 0)
    c = lax.broadcasted_iota(jnp.int32, (rows, cols), 1)
    return (row_of(r) == col_of(c)).astype(BF16)


def double_layer(tensor, pad):
    leg = tensor.shape[0]
    two = leg * leg
    phys = tensor.shape[4]
    big = two * pad

    def outer(first):
        def code(n):
            m, s = n // pad, n % pad
            a = m // leg if first else m % leg
            b = s // leg if first else s % leg
            return jnp.where(s < two, a * leg + b, -1)

        return code

    def same(n):
        return n

    total = None
    ket_rows = pick(big, two, outer(True), same)
    bra_rows = pick(big, two, outer(False), same)
    for p in range(phys):
        mat = tensor[:, :, :, :, p].reshape(two, two)
        ket_small = jnp.dot(ket_rows, mat, preferred_element_type=F32).astype(BF16)
        bra_small = jnp.dot(bra_rows, mat, preferred_element_type=F32).astype(BF16)
        ket = lax.dot_general(ket_small, ket_rows, (((1,), (1,)), ((), ())), preferred_element_type=F32)
        bra = lax.dot_general(bra_small, bra_rows, (((1,), (1,)), ((), ())), preferred_element_type=F32)
        total = ket * bra if total is None else total + ket * bra
    return total.astype(BF16)


def through_site(env, stacked, layer, pad):
    two = env.shape[2]
    summed = jnp.einsum("abm,asc->bmsc", env, stacked, preferred_element_type=F32).astype(BF16)
    amount, columns = summed.shape[0], summed.shape[3]
    flat = summed.reshape(amount, two * pad, columns)
    out = jnp.einsum("tn,btc->bnc", layer, flat, preferred_element_type=F32).astype(BF16)
    return out.reshape(amount, two, pad, columns)


def shards(left_env, up_left, up_center, right_env, center, ket_tensor):
    env_local = left_env[0]
    left_iso = up_left[0]
    left_mid = up_center[0]
    env_right = right_env[0]
    bond_mat = center[0]
    site_ket = ket_tensor[0]
    chi_all = env_local.shape[0]
    leg_width = env_local.shape[2]
    pad = -(-leg_width // 8) * 8
    widen = ((0, 0), (0, pad - leg_width), (0, 0))
    rows = left_iso.shape[0]
    col_count = left_iso.shape[2]

    mid_all = lax.all_gather(left_mid, "chi", axis=0, tiled=True)
    iso_all = lax.all_gather(left_iso, "chi", axis=0, tiled=True)
    next_iso = from_behind(left_iso, "cell", -1)
    bra_iso = lax.all_gather(next_iso, "dl", axis=2, tiled=True)

    layer = double_layer(site_ket, pad)

    mixed = jnp.einsum("abm,ax->bmx", env_local, bond_mat, preferred_element_type=F32).astype(BF16)
    bond_term = jnp.einsum("bma,amc->bc", mixed, env_right, preferred_element_type=F32)
    bond_slots = lax.dynamic_update_slice(
        jnp.zeros((chi_all, chi_all), F32), bond_term, (lax.axis_index("chi") * rows, 0)
    )
    bond_full = lax.psum(bond_slots, ("chi", "dl")).astype(BF16)

    right_cut = through_site(env_local, jnp.pad(mid_all, widen), layer, pad)
    center_term = jnp.einsum(
        "bmda,amc->bdc", right_cut[:, :, :leg_width], env_right, preferred_element_type=F32
    ).astype(BF16)
    iso_all, center_term = lax.optimization_barrier((iso_all, center_term))
    center_part = lax.psum_scatter(center_term, "dl", scatter_dimension=0, tiled=True)
    cross = lax.psum(
        jnp.einsum("bdc,bdy->cy", center_part, center_part, preferred_element_type=F32),
        ("chi", "dl"),
    )
    center_all = lax.all_gather(center_part, "dl", axis=0, tiled=True)

    left_cut = through_site(env_local, jnp.pad(iso_all, widen), layer, pad)
    env_term = jnp.einsum(
        "bmdc,bdk->kmc", left_cut[:, :, :leg_width], bra_iso, preferred_element_type=F32
    ).astype(BF16)
    env_new = lax.psum_scatter(env_term, "chi", scatter_dimension=0, tiled=True).astype(F32)

    bond_wide = bond_full.astype(F32)
    gram = jnp.dot(
        jnp.dot(bond_wide, cross, precision=HIGH), bond_wide.T, precision=HIGH
    )
    one = jnp.eye(chi_all, dtype=F32)
    norm_sum = jnp.sum(gram * one)
    factor = 0.25 * math.sqrt(chi_all) / jnp.sqrt(norm_sum)
    gram = gram * (factor * factor)
    product = None
    for sweep_index in range(ITERS):
        step = 1.5 * one - 0.5 * gram
        product = step if product is None else jnp.dot(product, step, precision=HIGH)
        if sweep_index < ITERS - 1:
            gram = jnp.dot(jnp.dot(step, gram, precision=HIGH), step, precision=HIGH)
    mine = lax.dynamic_slice_in_dim(product, lax.axis_index("dl") * col_count, col_count, 1)
    weight = lax.dot_general(bond_wide, mine, (((0,), (0,)), ((), ())), precision=HIGH)
    weight = weight * (factor * math.sqrt(chi_all * leg_width))
    new_left = jnp.einsum("bdc,cx->bdx", center_all.astype(F32), weight, precision=HIGH)
    return (env_new[None], new_left[None])


def solution(mesh):
    placed = (
        P("cell", None, "chi", None),
        P("cell", "chi", None, "dl"),
        P("cell", "chi", None, "dl"),
        P("cell", "dl", None, None),
        P("cell", None, "dl"),
        P("cell", None, None, None, None, None),
    )
    return jax.shard_map(
        shards,
        mesh=mesh,
        in_specs=placed,
        out_specs=(P("cell", "chi", None, "dl"), P("cell", "chi", None, "dl")),
        check_vma=False,
    )
```

time: 1730 us -> 747 us (0.43)
  waiting for transfers between devices: 976 us -> 123 us
  local copies, waits for them, and re-layouts: 252 us -> 133 us
  matrix products: 408 us -> 364 us
  blocking collectives: 61.2 us -> 100 us
    all_gather x8 -> x3, waiting for transfers between devices: 532 us -> 106 us  [the longest x1 87.6 us: shards(): center_all = lax.all_gather(center_part, 'dl', axis=0, tiled=True)]
    psum x5 -> x1, waiting for transfers between devices: 179 us -> 0.02 us  [shards(): lax.psum(jnp.einsum('bdc,bdy->cy', center_part, center_part, preferred_el...]
    reduce_scatter x1, waiting for transfers between devices: 154 us -> 0.01 us  [shards(): lax.psum_scatter(center_term, 'dl', scatter_dimension=0, tiled=True)]
    reduce_scatter x2 -> x0, waiting for transfers between devices: 108 us -> none  [the longest x1 88 us: shards(): lax.psum_scatter(jnp.einsum('bmdc,bdk->kmc', left_cut, bra_iso, preferred...]
    dynamic_slice x32 -> x0, local copies, waits for them, and re-layouts: 61.6 us -> none  [through_site(): finished = lax.map(partial(layered, tensor=tensor), blocks)]
    psum x1, blocking collectives: 38.9 us -> 100 us  [shards(): bond_full = lax.psum(bond_slots, ('chi', 'dl')).astype(BF16)]
    dynamic_update_slice x32 -> x0, local copies, waits for them, and re-layouts: 57.6 us -> none  [through_site(): finished = lax.map(partial(layered, tensor=tensor), blocks)]
    dot_general x80 -> x28, matrix products: 408 us -> 364 us  [the longest x2 164 us: through_site(): jnp.einsum('tn,btc->bnc', layer, flat, preferred_element_type=F32)]
  transfers between devices with their start and end apart: 18 -> 8, of which waited for: 15 -> 4; matrix products, arithmetic and copies ran while one was open for 19% -> 66% of each run, Pallas kernels for 0% -> 0%
where the time goes in v1:
time: 747 us; the launch traced here: 735 us
  matrix products  364 us (49%)
  local copies, waits for them, and re-layouts  133 us (18%)
  waiting for transfers between devices  123 us (16%)
  blocking collectives  100 us (13%)
  between operations  15.5 us (2%)
    dot_general x2, matrix products, through_site(): jnp.einsum('tn,btc->bnc', layer, flat, preferred_element_type=F32)  164 us
    convert_element_type x2, local copies, waits for them, and re-layouts, through_site(): jnp.einsum('abm,asc->bmsc', env, stacked, preferred_element_type=F32)  114 us
    psum x1, blocking collectives, shards(): bond_full = lax.psum(bond_slots, ('chi', 'dl')).astype(BF16)  100 us
    all_gather x1, waiting for transfers between devices, shards(): center_all = lax.all_gather(center_part, 'dl', axis=0, tiled=True)  87.6 us
    dot_general x2, matrix products, through_site(): jnp.einsum('abm,asc->bmsc', env, stacked, preferred_element_type=F32)  65.4 us
    dot_general x1, matrix products, shards(): jnp.einsum('bmdc,bdk->kmc', left_cut[:, :, :leg_width], bra_iso, preferre...  33.6 us
    dot_general x1, matrix products, shards(): jnp.einsum('bmda,amc->bdc', right_cut[:, :, :leg_width], env_right, prefe...  28.7 us
    dot_general x2, matrix products, double_layer(): lax.dot_general(bra_small, bra_rows, (((1,), (1,)), ((), ())), preferred_...  24 us
  transfers between devices with their start and end apart: 8, of which 4 were waited for; matrix products, arithmetic and copies ran while one was open for 66% of the time, Pallas kernels for 0%

profile of v1, /device:TPU:0, one launch (start us, length us, event | category | flops | bytes accessed | tf_op | source)
XLA Modules:
  0.0 735.4 jit_solution(9040913470576968549)
XLA Ops:
  7.2 0.0 copy-start
  7.2 0.0 all-gather.13.cloned.1.call-start
  7.2 2.4 copy.25
  9.6 0.0 all-gather.13.cloned.1.call-update
  9.7 0.0 all-gather.11.cloned.1.call-start
  9.7 2.4 copy.24
  12.1 0.0 all-gather.11.cloned.1.call-update
  12.1 0.0 reduce-scatter.5.cloned.1.call-start
  12.2 0.6 slice_reduce_fusion
  12.9 0.1 reshape_squeeze.6
  13.0 7.4 %fusion.45 = f32[1440,1440]{1,0:T(8,128)} fusion(bf16[36,36]{1,0:T(8,128)(2,1)S(1)} %reshape_squeeze.6, s32[1440]{0:T(1024)S(1)} %get-tuple-element.16, s32[1440]{0:T(1024)S(1)} %get-tuple-element.19, s32[1440]{0:T(1024)S(1)} %get-tuple-element.17, s32[1440]{0:T(1024)S(1)} %get-tuple-element.18, pred[1440]{0:T(1024)(128)(4,1)S(1)} %get-tuple-element.20, ...), kind=kOutput, calls=%fused_computation.59 | convolution fusion | flops 155468160 | bytes 8322912 | tf_op jit(solution)/shard_map/dot_general | solution.py:53
  20.3 11.2 %convolution_multiply_fusion.1 = f32[1440,1440]{1,0:T(8,128)} fusion(f32[1440,1440]{1,0:T(8,128)} %fusion.45, bf16[36,36]{1,0:T(8,128)(2,1)S(1)} %reshape_squeeze.6, s32[1440]{0:T(1024)S(1)} %get-tuple-element.16, s32[1440]{0:T(1024)S(1)} %get-tuple-element.19, s32[1440]{0:T(1024)S(1)} %get-tuple-element.17, s32[1440]{0:T(1024)S(1)} %get-tuple-element.18, ...), kind=kOutput, calls=%fused_computation.10 | convolution fusion | flops 157127040 | bytes 16617312 | tf_op jit(solution)/shard_map/dot_general | solution.py:54
  31.6 0.1 reshape_squeeze.7
  31.7 7.3 fusion.46
  39.0 12.8 %fusion.6 = bf16[1440,1440,1]{1,0,2:T(8,128)(2,1)} fusion(f32[1440,1440]{1,0:T(8,128)} %convolution_multiply_fusion.1, f32[1440,1440]{1,0:T(8,128)} %fusion.46, bf16[36,36]{1,0:T(8,128)(2,1)S(1)} %reshape_squeeze.7, s32[1440]{0:T(1024)S(1)} %get-tuple-element.16, s32[1440]{0:T(1024)S(1)} %get-tuple-element.19, s32[1440]{0:T(1024)S(1)} %get-tuple-element.17, ...), kind=kOutput, calls=%fused_computation.14 | convolution fusion | flops 161274240 | bytes 20764512 | tf_op jit(solution)/shard_map/dot_general | solution.py:54
  51.8 18.3 %all-gather.13.cloned.1.call-done = bf16[1,512,36,128]{1,3,2,0:T(8,128)(2,1)} async-done(((bf16[1,128,36,128]{1,3,2,0:T(8,128)(2,1)}), bf16[1,512,36,128]{1,3,2,0:T(8,128)(2,1)}) %all-gather.13.cloned.1.call-update) | async-done | bytes 4718608 | tf_op jit(solution)/shard_map/all_gather | solution.py:82
  70.1 32.3 %convert_bitcast_fusion.1 = bf16[128,36,40,128]{0,3,1,2:T(8,128)(2,1)} fusion(bf16[512,36,128]{0,2,1:T(8,128)(2,1)} %bitcast.128, bf16[1,512,128,36]{2,1,3,0:T(8,128)(2,1)} %param.6), kind=kOutput, calls=%fused_computation.1 | convolution fusion | flops 24182784000 | bytes 56623104 | tf_op jit(solution)/shard_map/abm,asc->bmsc/dot_general | solution.py:61
  102.4 57.2 %copy.26 = bf16[128,36,40,128]{3,2,1,0:T(8,128)(2,1)} copy(bf16[128,36,40,128]{0,3,1,2:T(8,128)(2,1)} %convert_bitcast_fusion.1) | data formatting | bytes 94371840 | tf_op jit(solution)/shard_map/convert_element_type | solution.py:61
  159.5 81.9 %convolution_convert_fusion.1 = bf16[128,128,1440]{1,2,0:T(8,128)(2,1)} fusion(bf16[128,1440,128]{2,1,0:T(8,128)(2,1)} %bitcast.122, bf16[1440,1440,1]{1,0,2:T(8,128)(2,1)} %fusion.6), kind=kOutput, calls=%fused_computation.7 | convolution fusion | flops 67971317760 | bytes 98519040 | tf_op jit(solution)/shard_map/tn,btc->bnc/dot_general | solution.py:64
  241.4 28.7 %bitcast_convert_fusion.1 = bf16[128,36,512]{2,0,1:T(8,128)(2,1)} fusion(bf16[1,128,36,512]{3,1,2,0:T(8,128)(2,1)S(1)} %copy-done.4, bf16[128,36,36,128]{3,2,1,0:T(8,128)(2,1)} %bitcast.130), kind=kOutput, calls=%fused_computation.12 | convolution fusion | flops 21745631232 | bytes 51904512 | tf_op jit(solution)/shard_map/bmda,amc->bdc/dot_general | solution.py:97
  270.2 0.0 reduce-scatter.5.cloned.1.call-update
  270.2 0.0 all-gather.7.cloned.1.call-start
  270.2 1.2 copy-done.1
  271.4 0.0 collective-permute-start
  271.4 2.8 collective-permute-done
  274.3 1.0 copy-done.2
  275.3 0.0 all-gather.7.cloned.1.call-update
  275.3 0.0 all-reduce.5.cloned.1.call-start
  275.4 33.1 %convert_bitcast_fusion = bf16[128,36,40,128]{0,3,1,2:T(8,128)(2,1)} fusion(bf16[512,36,128]{0,2,1:T(8,128)(2,1)} %bitcast.127, bf16[1,512,128,36]{2,1,3,0:T(8,128)(2,1)} %param.6), kind=kOutput, calls=%fused_computation | convolution fusion | flops 24182784000 | bytes 56623104 | tf_op jit(solution)/shard_map/abm,asc->bmsc/dot_general | solution.py:61
  308.5 57.2 %copy.29 = bf16[128,36,40,128]{3,2,1,0:T(8,128)(2,1)} copy(bf16[128,36,40,128]{0,3,1,2:T(8,128)(2,1)} %convert_bitcast_fusion) | data formatting | bytes 94371840 | tf_op jit(solution)/shard_map/convert_element_type | solution.py:61
  365.7 82.3 %convolution_convert_fusion = bf16[128,128,1440]{1,2,0:T(8,128)(2,1)} fusion(bf16[128,1440,128]{2,1,0:T(8,128)(2,1)} %bitcast.121, bf16[1440,1440,1]{1,0,2:T(8,128)(2,1)} %fusion.6), kind=kOutput, calls=%fused_computation.6 | convolution fusion | flops 67971317760 | bytes 98519040 | tf_op jit(solution)/shard_map/tn,btc->bnc/dot_general | solution.py:64
  448.0 3.5 convolution_bitcast_fusion.1
  451.4 0.0 all-reduce.5.cloned.1.call-update
  451.4 0.0 reduce-scatter.7.cloned.1.call-start
  451.5 0.0 all-gather.7.cloned.1.call-done
  451.5 33.6 %bitcast_convert_fusion = bf16[36,128,512]{2,1,0:T(8,128)(2,1)} fusion(bf16[128,36,512]{2,0,1:T(8,128)(2,1)} %all-gather.7.cloned.1.call-done, bf16[128,36,36,128]{3,2,1,0:T(8,128)(2,1)} %bitcast.129), kind=kOutput, calls=%fused_computation.11 | convolution fusion | flops 21745631232 | bytes 51904512 | tf_op jit(solution)/shard_map/bmdc,bdk->kmc/dot_general | solution.py:109
  485.1 6.7 copy.45
  491.9 0.0 reduce-scatter.7.cloned.1.call-update
  491.9 0.0 all-gather.9.cloned.1.call-start
  491.9 0.7 all-gather.9.cloned.1.call-update
  492.7 0.1 broadcast_in_dim.17
  492.8 6.6 fusion.42
  499.4 100.3 %all-reduce.6 = bf16[512,512]{1,0:T(8,128)(2,1)S(1)} all-reduce(f32[512,512]{1,0:T(8,128)S(1)} %fusion.42), channel_id=1, replica_groups=mesh['chi'=4,'dl'=4,'cell'=2] {'chi','dl'}, use_global_device_ids=true, to_apply=%region_2.3 | all-reduce | flops 262144 | bytes 1572864 | tf_op jit(solution)/shard_map/psum | solution.py:94
  599.6 0.0 all-reduce.5.cloned.1.call-done
  599.7 2.0 fusion.171
  601.6 1.3 select_reduce_fusion
  603.7 1.0 fusion.51
  604.7 1.1 fusion.50
  605.8 1.0 fusion.53
  606.8 1.1 fusion.49
  607.9 1.0 fusion.52
  608.9 1.0 fusion.55
  609.9 1.0 fusion.54
  611.0 1.0 fusion.47
  612.0 1.0 select_subtract_fusion
  613.0 1.0 fusion.56
  614.1 1.3 fusion.48
  615.4 1.0 fusion.170
  616.4 0.5 fusion.38
  616.9 13.8 %reduce-scatter.7.cloned.1.call-done = bf16[128,4608]{1,0:T(8,128)(2,1)} async-done(((bf16[512,4608]{1,0:T(8,128)(2,1)}), bf16[128,4608]{1,0:T(8,128)(2,1)}) %reduce-scatter.7.cloned.1.call-update) | async-done | bytes 1179664
  630.7 1.7 copy.46
  632.4 1.7 copy.33
  634.2 87.6 %all-gather.9.cloned.1.call-done = bf16[128,36,512]{2,0,1:T(8,128)(2,1)} async-done(((bf16[32,36,512]{2,0,1:T(8,128)(2,1)}), bf16[128,36,512]{2,0,1:T(8,128)(2,1)}) %all-gather.9.cloned.1.call-update) | async-done | bytes 4718608 | tf_op jit(solution)/shard_map/all_gather | solution.py:106
  721.7 6.4 convolution_bitcast_fusion
  (12 shorter events, 0.0 us)
Async XLA Ops:
  7.2 485.6 %copy-start = (bf16[1,512,128]{2,1,0:T(8,128)(2,1)S(1)}, bf16[1,512,128]{2,1,0:T(8,128)(2,1)}, u32[]{:S(2)}) copy-start(bf16[1,512,128]{2,1,0:T(8,128)(2,1)} %param.10) | copy-start | bytes 393220
  7.2 5.0 copy-start.3
  7.2 62.9 %all-gather.13.cloned.1.call-start = ((), (), s32[]{:S(2)}) async-start(), calls=%async_computation.7 | async-start | bytes 5898240 | tf_op jit(solution)/shard_map/all_gather | solution.py:82
  9.7 260.5 %all-gather.11.cloned.1.call-start = ((), (), s32[]{:S(2)}) async-start(), calls=%async_computation.6 | async-start | bytes 5898240 | tf_op jit(solution)/shard_map/all_gather | solution.py:83
  12.1 435.8 %reduce-scatter.5.cloned.1.call-start = ((), (), s32[]{:S(2)}) async-start(), calls=%async_computation.3 | async-start | bytes 5898240 | tf_op jit(solution)/shard_map/reduce_scatter | solution.py:101
  159.5 81.9 %copy-start.4 = (bf16[1,128,36,512]{3,1,2,0:T(8,128)(2,1)S(1)}, bf16[1,128,36,512]{3,1,2,0:T(8,128)(2,1)}, u32[]{:S(2)}) copy-start(bf16[1,128,36,512]{3,1,2,0:T(8,128)(2,1)} %param.9) | copy-start | bytes 14155780
  270.2 1.3 copy-start.1
  270.2 181.3 %all-gather.7.cloned.1.call-start = ((), (), s32[]{:S(2)}) async-start(), calls=%async_computation.2 | async-start | bytes 5898240 | tf_op jit(solution)/shard_map/all_gather | solution.py:85
  271.4 2.8 collective-permute-start
  274.3 1.0 copy-start.2
  275.3 324.3 %all-reduce.5.cloned.1.call-start = ((), (), s32[]{:S(2)}) async-start(), calls=%async_computation.5 | async-start | bytes 2097152 | tf_op jit(solution)/shard_map/psum | solution.py:102
  451.4 179.3 %reduce-scatter.7.cloned.1.call-start = ((), (), s32[]{:S(2)}) async-start(), calls=%async_computation.8 | async-start | bytes 5898240
  491.9 229.8 %all-gather.9.cloned.1.call-start = ((), (), s32[]{:S(2)}) async-start(), calls=%async_computation.4 | async-start | bytes 5898240 | tf_op jit(solution)/shard_map/all_gather | solution.py:106
Sparse Core Ops, SparseCore 0:
  10.4 59.6 all-gather.12
  72.5 56.9 all-gather.10
  270.3 85.2 reduce-scatter.4
  357.6 89.6 all-gather.6
  453.0 112.6 all-reduce.4
  568.5 62.1 reduce-scatter.6
  632.3 89.4 all-gather.8

commit v2 on v1

--- a/solution.py
+++ b/solution.py
@@ -3,6 +3,7 @@
 import jax
 import jax.numpy as jnp
 from jax import lax
+from jax.experimental.layout import Layout, with_layout_constraint
 from jax.sharding import PartitionSpec as P
 
 ITERS = 5
@@ -56,13 +57,25 @@
     return total.astype(BF16)
 
 
-def through_site(env, stacked, layer, pad):
-    two = env.shape[2]
-    summed = jnp.einsum("abm,asc->bmsc", env, stacked, preferred_element_type=F32).astype(BF16)
-    amount, columns = summed.shape[0], summed.shape[3]
-    flat = summed.reshape(amount, two * pad, columns)
-    out = jnp.einsum("tn,btc->bnc", layer, flat, preferred_element_type=F32).astype(BF16)
-    return out.reshape(amount, two, pad, columns)
+def row_major(block):
+    return with_layout_constraint(block, Layout(major_to_minor=tuple(range(block.ndim))))
+
+
+def site_input(env, stacked):
+    summed = jnp.einsum("abm,csa->cmsb", env, stacked, preferred_element_type=F32).astype(BF16)
+    summed = row_major(summed)
+    columns, two, pad, amount = summed.shape
+    return summed.reshape(columns, two * pad, amount)
+
+
+def site_output(flat, layer, pad):
+    out = jnp.einsum("tn,ctb->cnb", layer, flat, preferred_element_type=F32).astype(BF16)
+    return out.reshape(out.shape[0], out.shape[1] // pad, pad, out.shape[2])
+
+
+def spread_rows(block, pad):
+    turned = jnp.pad(block.transpose(2, 1, 0), ((0, 0), (0, pad - block.shape[1]), (0, 0)))
+    return lax.all_gather(row_major(turned), "chi", axis=2, tiled=True)
 
 
 def shards(left_env, up_left, up_center, right_env, center, ket_tensor):
@@ -75,12 +88,11 @@
     chi_all = env_local.shape[0]
     leg_width = env_local.shape[2]
     pad = -(-leg_width // 8) * 8
-    widen = ((0, 0), (0, pad - leg_width), (0, 0))
     rows = left_iso.shape[0]
     col_count = left_iso.shape[2]
 
-    mid_all = lax.all_gather(left_mid, "chi", axis=0, tiled=True)
-    iso_all = lax.all_gather(left_iso, "chi", axis=0, tiled=True)
+    mid_all = spread_rows(left_mid, pad)
+    iso_all = spread_rows(left_iso, pad)
     next_iso = from_behind(left_iso, "cell", -1)
     bra_iso = lax.all_gather(next_iso, "dl", axis=2, tiled=True)
 
@@ -91,25 +103,34 @@
     bond_slots = lax.dynamic_update_slice(
         jnp.zeros((chi_all, chi_all), F32), bond_term, (lax.axis_index("chi") * rows, 0)
     )
-    bond_full = lax.psum(bond_slots, ("chi", "dl")).astype(BF16)
+    mid_all, bond_slots = lax.optimization_barrier((mid_all, bond_slots))
+    bond_sum = lax.psum(bond_slots, ("chi", "dl"))
 
-    right_cut = through_site(env_local, jnp.pad(mid_all, widen), layer, pad)
+    right_cut = site_output(site_input(env_local, mid_all), layer, pad)
     center_term = jnp.einsum(
-        "bmda,amc->bdc", right_cut[:, :, :leg_width], env_right, preferred_element_type=F32
+        "amdb,amc->bdc", right_cut[:, :, :leg_width], env_right, preferred_element_type=F32
     ).astype(BF16)
-    iso_all, center_term = lax.optimization_barrier((iso_all, center_term))
+    iso_all, center_term, bond_sum = lax.optimization_barrier((iso_all, center_term, bond_sum))
+    bond_full = bond_sum.astype(BF16)
     center_part = lax.psum_scatter(center_term, "dl", scatter_dimension=0, tiled=True)
-    cross = lax.psum(
-        jnp.einsum("bdc,bdy->cy", center_part, center_part, preferred_element_type=F32),
-        ("chi", "dl"),
+    cross_part = jnp.einsum("bdc,bdy->cy", center_part, center_part, preferred_element_type=F32)
+
+    def env_piece(cut):
+        term = jnp.einsum(
+            "cmdb,bdk->kmc", cut[:, :, :leg_width], bra_iso, preferred_element_type=F32
+        ).astype(BF16)
+        return lax.psum_scatter(term, "chi", scatter_dimension=0, tiled=True).astype(F32)
+
+    half = (leg_width // 2) * pad
+    left_flat = site_input(env_local, iso_all)
+    left_early = site_output(left_flat, layer[:, :half], pad)
+    left_early, left_flat, cross_part, center_part = lax.optimization_barrier(
+        (left_early, left_flat, cross_part, center_part)
     )
+    cross = lax.psum(cross_part, ("chi", "dl"))
     center_all = lax.all_gather(center_part, "dl", axis=0, tiled=True)
-
-    left_cut = through_site(env_local, jnp.pad(iso_all, widen), layer, pad)
-    env_term = jnp.einsum(
-        "bmdc,bdk->kmc", left_cut[:, :, :leg_width], bra_iso, preferred_element_type=F32
-    ).astype(BF16)
-    env_new = lax.psum_scatter(env_term, "chi", scatter_dimension=0, tiled=True).astype(F32)
+    left_late = site_output(left_flat, layer[:, half:], pad)
+    env_new = jnp.concatenate([env_piece(left_early), env_piece(left_late)], axis=1)
 
     bond_wide = bond_full.astype(F32)
     gram = jnp.dot(

time: 747 us -> 810 us (1.084)
  waiting for transfers between devices: 123 us -> 286 us
  local copies, waits for them, and re-layouts: 133 us -> 19.4 us
  matrix products: 364 us -> 379 us
    convert_element_type x2 -> x0, local copies, waits for them, and re-layouts: 114 us -> none  [through_site(): jnp.einsum('abm,asc->bmsc', env, stacked, preferred_element_type=F32)]
    psum x1, waiting for transfers between devices: 0.02 us -> 77.7 us  [shards(): cross = lax.psum(cross_part, ('chi', 'dl'))]
    unnamed x8 -> x10, waiting for transfers between devices: 14.6 us -> 63 us
    all_gather x1, waiting for transfers between devices: 0.02 us -> 41.3 us  [shards(): bra_iso = lax.all_gather(next_iso, 'dl', axis=2, tiled=True)]
    dot_general x6 -> x8, matrix products: 292 us -> 308 us  [the longest x3 174 us: site_output(): jnp.einsum('tn,ctb->cnb', layer, flat, preferred_element_type=F32)]
    unnamed x15 -> x23, local copies, waits for them, and re-layouts: 17.2 us -> 16.1 us
  transfers between devices with their start and end apart: 8 -> 9, of which waited for: 4 -> 7; matrix products, arithmetic and copies ran while one was open for 66% -> 48% of each run, Pallas kernels for 0% -> 0%
where the time goes in v2:
time: 810 us; the launch traced here: 800 us
  matrix products  379 us (47%)
  waiting for transfers between devices  286 us (35%)
  blocking collectives  98.4 us (12%)
  local copies, waits for them, and re-layouts  19.4 us (2%)
  between operations  15.5 us (2%)
    dot_general x3, matrix products, site_output(): jnp.einsum('tn,ctb->cnb', layer, flat, preferred_element_type=F32)  174 us
    psum x1, blocking collectives, shards(): bond_sum = lax.psum(bond_slots, ('chi', 'dl'))  98.4 us
    all_gather x1, waiting for transfers between devices, shards(): center_all = lax.all_gather(center_part, 'dl', axis=0, tiled=True)  85.7 us
    psum x1, waiting for transfers between devices, shards(): cross = lax.psum(cross_part, ('chi', 'dl'))  77.7 us
    dot_general x2, matrix products, site_input(): jnp.einsum('abm,csa->cmsb', env, stacked, preferred_element_type=F32)  64.8 us
    unnamed x10, waiting for transfers between devices  63 us
    all_gather x1, waiting for transfers between devices, shards(): bra_iso = lax.all_gather(next_iso, 'dl', axis=2, tiled=True)  41.3 us
    dot_general x1, matrix products, shards(): jnp.einsum('amdb,amc->bdc', right_cut[:, :, :leg_width], env_right, prefe...  37.6 us
  transfers between devices with their start and end apart: 9, of which 7 were waited for; matrix products, arithmetic and copies ran while one was open for 48% of the time, Pallas kernels for 0%

profile of v2, /device:TPU:0, one launch (start us, length us, event | category | flops | bytes accessed | tf_op | source)
XLA Modules:
  0.0 800.2 jit_solution(4183132327198189968)
XLA Ops:
  7.2 0.0 all-gather.7.cloned.1.call-start
  7.2 2.2 copy.43
  9.5 1.2 pad.8
  10.7 0.0 all-gather.5.cloned.1.call-start
  10.8 1.3 copy.42
  12.1 1.2 pad.7
  13.3 0.0 reduce-scatter.8.cloned.1.call-start
  13.4 0.6 slice_reduce_fusion
  14.0 0.1 reshape_squeeze.6
  14.1 7.7 fusion.52
  21.8 11.0 %convolution_multiply_fusion.1 = f32[1440,1440]{1,0:T(8,128)} fusion(f32[1440,1440]{1,0:T(8,128)} %fusion.52, bf16[36,36]{1,0:T(8,128)(2,1)S(1)} %reshape_squeeze.6, s32[1440]{0:T(1024)S(1)} %get-tuple-element.30, s32[1440]{0:T(1024)S(1)} %get-tuple-element.33, s32[1440]{0:T(1024)S(1)} %get-tuple-element.31, s32[1440]{0:T(1024)S(1)} %get-tuple-element.32, ...), kind=kOutput, calls=%fused_computation.13 | convolution fusion | flops 157127040 | bytes 16617312 | tf_op jit(solution)/shard_map/dot_general | solution.py:55
  32.9 0.1 reshape_squeeze.7
  33.0 7.3 fusion.53
  40.3 12.5 %fusion.7 = bf16[1440,1440]{1,0:T(8,128)(2,1)} fusion(f32[1440,1440]{1,0:T(8,128)} %convolution_multiply_fusion.1, f32[1440,1440]{1,0:T(8,128)} %fusion.53, bf16[36,36]{1,0:T(8,128)(2,1)S(1)} %reshape_squeeze.7, s32[1440]{0:T(1024)S(1)} %get-tuple-element.30, s32[1440]{0:T(1024)S(1)} %get-tuple-element.33, s32[1440]{0:T(1024)S(1)} %get-tuple-element.31, ...), kind=kOutput, calls=%fused_computation.15 | convolution fusion | flops 161274240 | bytes 20764512 | tf_op jit(solution)/shard_map/dot_general | solution.py:55
  52.8 0.1 broadcast_in_dim.15
  52.9 6.5 fusion.49
  59.5 15.4 %all-gather.7.cloned.1.call-done = bf16[128,40,512]{2,1,0:T(8,128)(2,1)} async-done(((bf16[128,40,128]{2,1,0:T(8,128)(2,1)}), bf16[128,40,512]{2,1,0:T(8,128)(2,1)}) %all-gather.7.cloned.1.call-update) | async-done | bytes 5242896 | tf_op jit(solution)/shard_map/all_gather | solution.py:78
  74.8 32.4 %convolution_convert_fusion.2 = bf16[128,40,128,36]{2,1,3,0:T(8,128)(2,1)} fusion(bf16[128,40,512]{2,1,0:T(8,128)(2,1)} %all-gather.7.cloned.1.call-done, bf16[1,512,128,36]{2,1,3,0:T(8,128)(2,1)} %param.6), kind=kOutput, calls=%fused_computation.4 | convolution fusion | flops 24182784000 | bytes 57147392 | tf_op jit(solution)/shard_map/abm,csa->cmsb/dot_general | solution.py:65
  107.2 98.4 %all-reduce.6 = bf16[512,512]{1,0:T(8,128)(2,1)} all-reduce(f32[512,512]{1,0:T(8,128)S(1)} %fusion.49), channel_id=1, replica_groups=mesh['chi'=4,'dl'=4,'cell'=2] {'chi','dl'}, use_global_device_ids=true, to_apply=%region_0.1 | all-reduce | flops 262144 | bytes 1572864 | tf_op jit(solution)/shard_map/psum | solution.py:107
  205.6 81.7 %convolution_convert_fusion = bf16[128,128,1440]{1,2,0:T(8,128)(2,1)} fusion(bf16[128,1440,128]{2,1,0:T(8,128)(2,1)} %bitcast.157, bf16[1440,1440]{1,0:T(8,128)(2,1)} %fusion.7), kind=kOutput, calls=%fused_computation.2 | convolution fusion | flops 67971317760 | bytes 98519040 | tf_op jit(solution)/shard_map/tn,ctb->cnb/dot_general | solution.py:72
  287.3 37.6 %fusion.10 = bf16[128,36,512]{2,0,1:T(8,128)(2,1)} fusion(bf16[1,128,36,512]{3,1,2,0:T(8,128)(2,1)S(1)} %copy-done.7, bf16[128,36,36,128]{3,2,1,0:T(8,128)(2,1)} %bitcast.158), kind=kOutput, calls=%fused_computation.18 | convolution fusion | flops 21745631232 | bytes 51904512 | tf_op jit(solution)/shard_map/amdb,amc->bdc/dot_general | solution.py:110
  324.9 0.0 reduce-scatter.8.cloned.1.call-update
  324.9 0.0 all-gather.9.cloned.1.call-start
  325.0 1.2 copy-done.4
  326.2 2.8 collective-permute-done
  329.0 1.0 copy-done.5
  330.1 0.0 all-reduce.5.cloned.1.call-start
  330.1 32.4 %convolution_convert_fusion.1 = bf16[128,40,128,36]{2,1,3,0:T(8,128)(2,1)} fusion(bf16[128,40,512]{2,1,0:T(8,128)(2,1)} %all-gather.5.cloned.1.call-done, bf16[1,512,128,36]{2,1,3,0:T(8,128)(2,1)} %param.6), kind=kOutput, calls=%fused_computation.3 | convolution fusion | flops 24182784000 | bytes 57147392 | tf_op jit(solution)/shard_map/abm,csa->cmsb/dot_general | solution.py:65
  362.5 45.4 %convolution_convert_fusion.4 = bf16[128,128,720]{1,2,0:T(8,128)(2,1)} fusion(bf16[128,1440,128]{2,1,0:T(8,128)(2,1)} %bitcast.155, bf16[1440,1440]{1,0:T(8,128)(2,1)} %fusion.7), kind=kOutput, calls=%fused_computation.10 | convolution fusion | flops 33985658880 | bytes 72990720 | tf_op jit(solution)/shard_map/tn,ctb->cnb/dot_general | solution.py:72
  408.0 3.6 convolution_bitcast_fusion.1
  411.6 46.5 %convolution_convert_fusion.3 = bf16[128,128,720]{1,2,0:T(8,128)(2,1)} fusion(bf16[128,1440,128]{2,1,0:T(8,128)(2,1)} %bitcast.156, bf16[1440,1440]{1,0:T(8,128)(2,1)} %fusion.7), kind=kOutput, calls=%fused_computation.9 | convolution fusion | flops 33985658880 | bytes 72990720 | tf_op jit(solution)/shard_map/tn,ctb->cnb/dot_general | solution.py:72
  458.1 0.0 reduce-scatter.12.cloned.1.call-start
  458.2 41.3 %all-gather.9.cloned.1.call-done = bf16[128,36,512]{2,0,1:T(8,128)(2,1)} async-done(((bf16[128,36,128]{2,0,1:T(8,128)(2,1)}), bf16[128,36,512]{2,0,1:T(8,128)(2,1)}) %all-gather.9.cloned.1.call-update) | async-done | bytes 4718608 | tf_op jit(solution)/shard_map/all_gather | solution.py:97
  499.4 15.8 %bitcast_convert_fusion.1 = bf16[128,18,512]{2,0,1:T(8,128)(2,1)S(1)} fusion(bf16[128,36,512]{2,0,1:T(8,128)(2,1)} %all-gather.9.cloned.1.call-done, bf16[128,18,36,128]{3,2,1,0:T(8,128)(2,1)} %bitcast.160), kind=kOutput, calls=%fused_computation.19 | convolution fusion | flops 10872815616 | bytes 28311552 | tf_op jit(solution)/shard_map/cmdb,bdk->kmc/dot_general | solution.py:119
  515.2 2.4 copy.82
  517.6 0.0 reduce-scatter.10.cloned.1.call-start
  517.7 15.8 %bitcast_convert_fusion.2 = bf16[128,18,512]{2,0,1:T(8,128)(2,1)S(1)} fusion(bf16[128,36,512]{2,0,1:T(8,128)(2,1)} %all-gather.9.cloned.1.call-done, bf16[128,18,40,128]{3,2,1,0:T(8,128)(2,1)} %bitcast.159), kind=kOutput, calls=%fused_computation.20 | convolution fusion | flops 10872815616 | bytes 30670848 | tf_op jit(solution)/shard_map/cmdb,bdk->kmc/dot_general | solution.py:119
  533.5 2.4 copy.80
  536.0 0.3 all-gather.11.cloned.1.call-start
  536.3 0.5 all-gather.11.cloned.1.call-update
  536.8 77.7 %all-reduce.5.cloned.1.call-done = f32[512,512]{1,0:T(8,128)} async-done(((f32[512,512]{1,0:T(8,128)}), f32[512,512]{1,0:T(8,128)}) %all-reduce.5.cloned.1.call-update) | async-done | bytes 1048592 | tf_op jit(solution)/shard_map/psum | solution.py:130
  614.5 2.0 fusion.176
  616.5 1.4 select_reduce_fusion
  618.5 1.0 fusion.58
  619.6 1.1 fusion.57
  620.6 1.0 fusion.60
  621.6 1.1 fusion.56
  622.7 1.0 fusion.59
  623.8 1.0 fusion.62
  624.8 1.0 fusion.61
  625.8 1.0 fusion.54
  626.9 1.0 select_subtract_fusion
  627.9 1.0 fusion.63
  628.9 1.3 fusion.55
  630.3 1.0 fusion.175
  631.3 0.5 fusion.45
  631.8 22.7 %reduce-scatter.12.cloned.1.call-done = bf16[128,2304]{1,0:T(8,128)(2,1)} async-done(((bf16[512,2304]{1,0:T(8,128)(2,1)}), bf16[128,2304]{1,0:T(8,128)(2,1)}) %reduce-scatter.12.cloned.1.call-update) | async-done | bytes 589840
  654.5 1.4 copy.83
  655.8 39.7 %reduce-scatter.10.cloned.1.call-done = bf16[128,2304]{1,0:T(8,128)(2,1)} async-done(((bf16[512,2304]{1,0:T(8,128)(2,1)}), bf16[128,2304]{1,0:T(8,128)(2,1)}) %reduce-scatter.10.cloned.1.call-update) | async-done | bytes 589840
  695.5 2.1 copy.81
  697.6 1.2 fusion.44
  698.9 2.0 copy.56
  700.8 85.7 %all-gather.11.cloned.1.call-done = bf16[128,36,512]{2,0,1:T(8,128)(2,1)} async-done(((bf16[32,36,512]{2,0,1:T(8,128)(2,1)}), bf16[128,36,512]{2,0,1:T(8,128)(2,1)}) %all-gather.11.cloned.1.call-update) | async-done | bytes 4718608 | tf_op jit(solution)/shard_map/all_gather | solution.py:131
  786.5 6.3 convolution_bitcast_fusion
  (26 shorter events, 0.2 us)
Async XLA Ops:
  7.2 45.8 %copy-start = (bf16[1,512,128]{2,1,0:T(8,128)(2,1)S(1)}, bf16[1,512,128]{2,1,0:T(8,128)(2,1)}, u32[]{:S(2)}) copy-start(bf16[1,512,128]{2,1,0:T(8,128)(2,1)} %param.10) | copy-start | bytes 393220
  7.2 3.6 copy-start.3
  7.2 67.6 %all-gather.7.cloned.1.call-start = ((), (), s32[]{:S(2)}) async-start(), calls=%async_computation.4 | async-start | bytes 6553600 | tf_op jit(solution)/shard_map/all_gather | solution.py:78
  9.5 3.9 copy-start.6
  10.7 314.2 %all-gather.5.cloned.1.call-start = ((), (), s32[]{:S(2)}) async-start(), calls=%async_computation.3 | async-start | bytes 6553600 | tf_op jit(solution)/shard_map/all_gather | solution.py:78
  13.3 394.7 %reduce-scatter.8.cloned.1.call-start = ((), (), s32[]{:S(2)}) async-start(), calls=%async_computation.5 | async-start | bytes 5898240 | tf_op jit(solution)/shard_map/reduce_scatter | solution.py:115
  205.6 81.7 %copy-start.7 = (bf16[1,128,36,512]{3,1,2,0:T(8,128)(2,1)S(1)}, bf16[1,128,36,512]{3,1,2,0:T(8,128)(2,1)}, u32[]{:S(2)}) copy-start(bf16[1,128,36,512]{3,1,2,0:T(8,128)(2,1)} %param.9) | copy-start | bytes 14155780
  324.9 1.3 copy-start.4
  324.9 174.5 %all-gather.9.cloned.1.call-start = ((), (), s32[]{:S(2)}) async-start(), calls=%async_computation.6 | async-start | bytes 5898240 | tf_op jit(solution)/shard_map/all_gather | solution.py:97
  326.2 2.8 collective-permute-start
  329.0 1.0 copy-start.5
  330.1 284.4 %all-reduce.5.cloned.1.call-start = ((), (), s32[]{:S(2)}) async-start(), calls=%async_computation.8 | async-start | bytes 2097152 | tf_op jit(solution)/shard_map/psum | solution.py:130
  458.1 196.4 %reduce-scatter.12.cloned.1.call-start = ((), (), s32[]{:S(2)}) async-start(), calls=%async_computation.10 | async-start | bytes 2949120
  517.6 177.9 %reduce-scatter.10.cloned.1.call-start = ((), (), s32[]{:S(2)}) async-start(), calls=%async_computation.9 | async-start | bytes 2949120
  533.5 81.0 %copy-start.2 = (bf16[512,512]{1,0:T(8,128)(2,1)S(1)}, bf16[512,512]{1,0:T(8,128)(2,1)}, u32[]{:S(2)}) copy-start(bf16[512,512]{1,0:T(8,128)(2,1)} %all-reduce.6) | copy-start | bytes 1572868
  536.0 250.5 %all-gather.11.cloned.1.call-start = ((), (), s32[]{:S(2)}) async-start(), calls=%async_computation.7 | async-start | bytes 5898240 | tf_op jit(solution)/shard_map/all_gather | solution.py:131
  698.9 94.0 %copy-start.1 = (bf16[1,512,128]{2,1,0:T(8,128)(2,1)S(1)}, bf16[1,512,128]{2,1,0:T(8,128)(2,1)}, u32[]{:S(2)}) copy-start(bf16[1,512,128]{2,1,0:T(8,128)(2,1)} %param.10) | copy-start | bytes 393220
Sparse Core Ops, SparseCore 0:
  10.8 63.9 all-gather.6
  77.2 69.7 all-gather.4
  325.1 82.6 reduce-scatter.7
  409.7 89.6 all-gather.8
  504.6 109.8 all-reduce.4
  618.0 36.4 reduce-scatter.11
  658.1 37.3 reduce-scatter.9
  697.1 89.3 all-gather.10
